TPU v7x, 32 devices: a whole 2x2x4 slice. The times are simulated.
32 devices in a mesh: dp: 8 (over z, y), rep: 4 (over x, core).
Axes of the slice: x: 2, y: 2, z: 4, core: 2. Of those that a mesh axis runs over, the one named last changes fastest.
Arguments:
- image_tokens: bfloat16 [256, 50, 768], P(('dp', 'rep')), may hold values from -6 to 6
- image_weights: bfloat16 [768, 9216], P('dp'), may hold values from -1 to 1
- image_vectors: float32 [9216], replicated, may hold values from -0.8 to 1.4
- text_tokens: bfloat16 [64, 64, 768], P(('dp', 'rep')), may hold values from -6 to 6
- segments: int32 [64, 64], P(('dp', 'rep')), may hold values from 0 to 3, never falling along the last dimension, each value on 1 to 28 neighbouring positions
- text_weights: float32 [768, 9216], P('dp'), may hold values from -1 to 1
- text_vectors: float32 [9216], replicated, may hold values from -0.8 to 1.4
- momentum: float32 [768, 9216], P('dp'), may hold values from -0.5 to 0.5
- vector_momentum: float32 [9216], replicated, may hold values from -2.5 to 2.5
- error_feedback: float32 [4, 768, 9216], P('rep', 'dp'), may hold values from -2.5 to 2.5
- start_factors: float32 [8, 9216], replicated, may hold values from -6 to 6
Outputs:
- contrast_loss: float32 [], replicated
- text_output: float32 [64, 64, 768], P(('dp', 'rep'))
- text_input_grad: float32 [64, 64, 768], P(('dp', 'rep'))
- new_weights: float32 [768, 9216], P('dp')
- new_momentum: float32 [768, 9216], P('dp')
- new_feedback: float32 [4, 768, 9216], P('rep', 'dp')
- new_vectors: float32 [9216], replicated
- new_vector_momentum: float32 [9216], replicated
- left_factors: float32 [32, 768], replicated
- right_factors: float32 [8, 9216], replicated
Inputs may be any that keep to these rules, and one draw needn't show every extreme that they name: `segments`: each row holds 4 captions numbered in order, each of 1 to 28 tokens, some caption of exactly 28.
All inputs are finite; a program needn't handle non-finite values.
Results may differ from a plain program's by a relative error of at most 0.015.
The roundings to bfloat16 on the way count: a program that leaves them out, or rounds other values in their place, can miss the bound.
Values may be sent and summed in bfloat16 or wider, within the bound.
A program may use at most 192 MiB of HBM per device.

v0:
```python
import jax
import jax.numpy as jnp
from jax import lax
from jax.sharding import PartitionSpec as P

D = 768
FF = 3072
HEADS = 12
HEAD_DIM = 64
PER_ROW = 4
PRECISE = lax.Precision.HIGHEST
LAYER_EPS = 1e-06
SCORE_SCALE = 0.125
LOGIT_SCALE = 50.0
MOMENTUM_DECAY = 0.9
STEP_RATE = 0.08
NORM_FLOOR = 1e-08
MASKED = -1e30


def layer_norm(values, layer_gain, layer_shift):
    center = values - jnp.mean(values, axis=-1, keepdims=True)
    spread = jnp.mean(center * center, axis=-1, keepdims=True)
    return center * lax.rsqrt(spread + LAYER_EPS) * layer_gain + layer_shift


def unit_rows(values):
    return values * lax.rsqrt(jnp.sum(values * values, axis=-1, keepdims=True) + LAYER_EPS)


def vector_parts(vectors):
    pieces = [vectors[position * D : (position + 1) * D] for position in range(8)]
    return pieces + [vectors[8 * D :]]


def matrix_bounds():
    return ((0, 3 * D), (3 * D, 4 * D), (4 * D, 4 * D + FF), (4 * D + FF, 4 * D + 2 * FF))


def row_log_total(values):
    highest = jnp.max(values, axis=1, keepdims=True)
    return highest[:, 0] + jnp.log(jnp.sum(jnp.exp(values - highest), axis=1))


def masked_scores(query_heads, key_heads, allowed):
    scores = (
        jnp.einsum("rshd,rthd->rhst", query_heads, key_heads, preferred_element_type=jnp.float32)
        * SCORE_SCALE
    )
    return jnp.where(allowed[:, None], scores, MASKED)


def block_forward(inputs, allowed, weights, vector_pieces):
    (
        gain_one,
        shift_one,
        bias_query,
        bias_value,
        bias_out,
        gain_two,
        shift_two,
        bias_shrink,
        bias_expand,
    ) = vector_pieces
    row_count, seq_tokens = (inputs.shape[0], inputs.shape[1])
    normed = layer_norm(inputs, gain_one, shift_one).astype(jnp.bfloat16)
    mixing = jnp.einsum(
        "rsd,dc->rsc", normed, weights[:, : 3 * D], preferred_element_type=jnp.float32
    )
    mixing = mixing + jnp.concatenate([bias_query, jnp.zeros_like(bias_query), bias_value])
    head_parts = mixing.astype(jnp.bfloat16).reshape(row_count, seq_tokens, 3, HEADS, HEAD_DIM)
    query_heads, key_heads, value_heads = (
        head_parts[:, :, 0],
        head_parts[:, :, 1],
        head_parts[:, :, 2],
    )
    scores = masked_scores(query_heads, key_heads, allowed)
    highest = jnp.max(scores, axis=-1, keepdims=True)
    log_total = highest + jnp.log(jnp.sum(jnp.exp(scores - highest), axis=-1, keepdims=True))
    attention = jnp.exp(scores - log_total).astype(jnp.bfloat16)
    mixed_heads = jnp.einsum(
        "rhst,rthd->rshd", attention, value_heads, preferred_element_type=jnp.float32
    )
    mixed_heads = mixed_heads.reshape(row_count, seq_tokens, D).astype(jnp.bfloat16)
    attended = (
        jnp.einsum(
            "rsd,de->rse",
            mixed_heads,
            weights[:, 3 * D : 4 * D],
            preferred_element_type=jnp.float32,
        )
        + bias_out
    )
    middle = inputs + attended
    normed_two = layer_norm(middle, gain_two, shift_two).astype(jnp.bfloat16)
    hidden = (
        jnp.einsum(
            "rsd,df->rsf",
            normed_two,
            weights[:, 4 * D : 4 * D + FF],
            preferred_element_type=jnp.float32,
        )
        + bias_expand
    )
    active = jax.nn.gelu(hidden, approximate=False).astype(jnp.bfloat16)
    shrunk = (
        jnp.einsum(
            "rsf,df->rsd", active, weights[:, 4 * D + FF :], preferred_element_type=jnp.float32
        )
        + bias_shrink
    )
    forward_kept = (
        normed,
        query_heads,
        key_heads,
        value_heads,
        log_total,
        mixed_heads,
        middle,
        normed_two,
        hidden,
        active,
    )
    return (middle + shrunk, forward_kept)


def token_sum(values_low):
    return jnp.sum(values_low.astype(jnp.float32).reshape(-1, values_low.shape[-1]), axis=0)


def block_backward(inputs, allowed, weights, vector_pieces, forward_kept, grad_out):
    (
        gain_one,
        shift_one,
        bias_query,
        bias_value,
        bias_out,
        gain_two,
        shift_two,
        bias_shrink,
        bias_expand,
    ) = vector_pieces
    (
        normed,
        query_heads,
        key_heads,
        value_heads,
        log_total,
        mixed_heads,
        middle,
        normed_two,
        hidden,
        active,
    ) = forward_kept
    row_count, seq_tokens = (inputs.shape[0], inputs.shape[1])
    grad_shrunk = grad_out.astype(jnp.bfloat16)
    grad_active = jnp.einsum(
        "rsd,df->rsf", grad_shrunk, weights[:, 4 * D + FF :], preferred_element_type=jnp.float32
    )
    _, gelu_back = jax.vjp(lambda before_gelu: jax.nn.gelu(before_gelu, approximate=False), hidden)
    grad_hidden = gelu_back(grad_active)[0].astype(jnp.bfloat16)
    grad_normed_two = jnp.einsum(
        "rsf,df->rsd",
        grad_hidden,
        weights[:, 4 * D : 4 * D + FF],
        preferred_element_type=jnp.float32,
    )
    _, norm_two_back = jax.vjp(layer_norm, middle, gain_two, shift_two)
    grad_middle, grad_gain_two, grad_shift_two = norm_two_back(grad_normed_two)
    grad_middle = grad_middle + grad_out
    grad_attended = grad_middle.astype(jnp.bfloat16)
    grad_mixed = jnp.einsum(
        "rse,de->rsd", grad_attended, weights[:, 3 * D : 4 * D], preferred_element_type=jnp.float32
    )
    grad_mixed = grad_mixed.astype(jnp.bfloat16).reshape(row_count, seq_tokens, HEADS, HEAD_DIM)
    attention = jnp.exp(masked_scores(query_heads, key_heads, allowed) - log_total)
    grad_values = jnp.einsum(
        "rhst,rshd->rthd",
        attention.astype(jnp.bfloat16),
        grad_mixed,
        preferred_element_type=jnp.float32,
    )
    grad_attention = jnp.einsum(
        "rshd,rthd->rhst", grad_mixed, value_heads, preferred_element_type=jnp.float32
    )
    grad_scores = attention * (
        grad_attention - jnp.sum(attention * grad_attention, axis=-1, keepdims=True)
    )
    grad_scores = grad_scores.astype(jnp.bfloat16)
    grad_query = (
        jnp.einsum("rhst,rthd->rshd", grad_scores, key_heads, preferred_element_type=jnp.float32)
        * SCORE_SCALE
    )
    grad_keys = (
        jnp.einsum("rhst,rshd->rthd", grad_scores, query_heads, preferred_element_type=jnp.float32)
        * SCORE_SCALE
    )
    grad_mixing = (
        jnp.stack([grad_query, grad_keys, grad_values], axis=2)
        .reshape(row_count, seq_tokens, 3 * D)
        .astype(jnp.bfloat16)
    )
    grad_normed = jnp.einsum(
        "rsc,dc->rsd", grad_mixing, weights[:, : 3 * D], preferred_element_type=jnp.float32
    )
    _, norm_one_back = jax.vjp(layer_norm, inputs, gain_one, shift_one)
    grad_inputs, grad_gain_one, grad_shift_one = norm_one_back(grad_normed)
    grad_inputs = grad_inputs + grad_middle
    vector_grad = jnp.concatenate(
        [
            grad_gain_one,
            grad_shift_one,
            token_sum(grad_mixing[..., :D]),
            token_sum(grad_mixing[..., 2 * D :]),
            token_sum(grad_attended),
            grad_gain_two,
            grad_shift_two,
            token_sum(grad_shrunk),
            token_sum(grad_hidden),
        ]
    )
    tokens = row_count * seq_tokens
    outer_terms = (
        (normed.reshape(tokens, D), grad_mixing.reshape(tokens, 3 * D)),
        (mixed_heads.reshape(tokens, D), grad_attended.reshape(tokens, D)),
        (normed_two.reshape(tokens, D), grad_hidden.reshape(tokens, FF)),
        (grad_shrunk.reshape(tokens, D), active.reshape(tokens, FF)),
    )
    return (grad_inputs, vector_grad, outer_terms)


def orthonormal(stacked):
    finished = []
    for column_id in range(stacked.shape[1]):
        vector = stacked[:, column_id]
        for earlier in finished:
            vector = vector - jnp.sum(earlier * vector, axis=-1, keepdims=True) * earlier
        vector = vector / (jnp.sqrt(jnp.sum(vector * vector, axis=-1, keepdims=True)) + NORM_FLOOR)
        finished.append(vector)
    return jnp.stack(finished, axis=1)


def rows_factor(start_part, row_block):
    return jnp.einsum("kc,dc->kd", start_part, row_block, precision=PRECISE)


def per_device(
    image_tokens,
    image_weights,
    image_vectors,
    text_tokens,
    segments,
    text_weights,
    text_vectors,
    momentum,
    vector_momentum,
    error_feedback,
    start_factors,
):
    rep_count = lax.axis_size("rep")
    device_pairs = image_tokens.shape[0]
    patches = image_tokens.shape[1]
    pair_total = device_pairs * lax.axis_size("dp") * rep_count
    own_rows = text_weights.shape[0]
    row_start = lax.axis_index("dp") * own_rows
    factor_rank = start_factors.shape[0]
    bounds = matrix_bounds()
    text_low, frozen = (
        lax.all_gather(text_weights.astype(jnp.bfloat16), "dp", axis=0, tiled=True),
        lax.all_gather(image_weights, "dp", axis=0, tiled=True),
    )
    full_mask = jnp.zeros((device_pairs, patches, patches), jnp.int32) == 0
    image_out, _ = block_forward(
        image_tokens.astype(jnp.float32), full_mask, frozen, vector_parts(image_vectors)
    )
    image_emb = unit_rows(jnp.mean(image_out, axis=1)).astype(jnp.bfloat16)
    text_float = text_tokens.astype(jnp.float32)
    allowed = segments[:, :, None] == segments[:, None, :]
    vector_pieces = vector_parts(text_vectors)
    text_output, forward_kept = block_forward(text_float, allowed, text_low, vector_pieces)
    caption_marks = (
        segments[:, None, :] == jnp.arange(PER_ROW, dtype=jnp.int32)[None, :, None]
    ).astype(jnp.float32)
    counts = jnp.sum(caption_marks, axis=-1, keepdims=True)
    pooled = (
        jnp.einsum("rks,rsd->rkd", caption_marks, text_output, precision=PRECISE) / counts
    ).reshape(-1, D)
    text_norm, embed_back = jax.vjp(unit_rows, pooled)
    text_emb = text_norm.astype(jnp.bfloat16)
    image_all, text_all = (
        lax.all_gather(image_emb, ("dp", "rep"), axis=0, tiled=True),
        lax.all_gather(text_emb, ("dp", "rep"), axis=0, tiled=True),
    )
    offset = lax.axis_index(("dp", "rep")) * device_pairs
    diagonal_pick = (
        jnp.arange(pair_total, dtype=jnp.int32)[None, :]
        == offset + jnp.arange(device_pairs, dtype=jnp.int32)[:, None]
    ).astype(jnp.float32)
    image_logits = LOGIT_SCALE * jnp.einsum(
        "pd,bd->pb", image_emb, text_all, preferred_element_type=jnp.float32
    )
    text_logits = LOGIT_SCALE * jnp.einsum(
        "pd,bd->pb", text_emb, image_all, preferred_element_type=jnp.float32
    )
    image_log_total = row_log_total(image_logits)
    text_log_total = row_log_total(text_logits)
    loss_part = (
        jnp.sum(image_log_total - jnp.sum(diagonal_pick * image_logits, axis=1))
        + jnp.sum(text_log_total - jnp.sum(diagonal_pick * text_logits, axis=1))
    ) / (2.0 * pair_total)
    text_soft = ((jnp.exp(text_logits - text_log_total[:, None]) - diagonal_pick) * 0.5).astype(
        jnp.bfloat16
    )
    grad_text = LOGIT_SCALE * jnp.einsum(
        "pb,bd->pd", text_soft, image_all, preferred_element_type=jnp.float32
    )
    log_totals = lax.all_gather(image_log_total, ("dp", "rep"), axis=0, tiled=True)
    column_soft = ((jnp.exp(text_logits - log_totals[None, :]) - diagonal_pick) * 0.5).astype(
        jnp.bfloat16
    )
    grad_text = grad_text + LOGIT_SCALE * jnp.einsum(
        "pb,bd->pd", column_soft, image_all, preferred_element_type=jnp.float32
    )
    grad_pooled = embed_back(grad_text)[0].reshape(-1, PER_ROW, D) / counts
    grad_out = jnp.einsum("rks,rkd->rsd", caption_marks, grad_pooled, precision=PRECISE)
    grad_inputs, vector_grad, outer_terms = block_backward(
        text_float, allowed, text_low, vector_pieces, forward_kept, grad_out
    )
    blocks = [
        jnp.einsum("tc,tk->ck", left_side, right_side, preferred_element_type=jnp.float32)
        for left_side, right_side in outer_terms
    ]
    grad_rows = lax.psum_scatter(
        jnp.concatenate(blocks, axis=1), "dp", scatter_dimension=0, tiled=True
    )
    feedback_rows = error_feedback[0]
    worker_rows = grad_rows + feedback_rows
    factor_rows = jnp.concatenate(
        [
            rows_factor(start_factors[:, first_col:after_col], worker_rows[:, first_col:after_col])
            for first_col, after_col in bounds
        ],
        axis=0,
    )
    gathered_rows = lax.all_gather(factor_rows, "dp", axis=1, tiled=True)
    factor = lax.psum(gathered_rows.astype(jnp.bfloat16), "rep").astype(jnp.float32)
    vector_total, loss_total = lax.psum((vector_grad, loss_part), ("dp", "rep"))
    left_basis = orthonormal(factor.reshape(4, factor_rank, D)).reshape(4 * factor_rank, D)
    basis_rows = lax.dynamic_slice_in_dim(left_basis, row_start, own_rows, 1)
    right_part = jnp.concatenate(
        [
            jnp.einsum(
                "kd,dc->kc",
                basis_rows[matrix_id * factor_rank : (matrix_id + 1) * factor_rank],
                worker_rows[:, bounds[matrix_id][0] : bounds[matrix_id][1]],
                precision=PRECISE,
            )
            for matrix_id in range(4)
        ],
        axis=1,
    )
    new_right = lax.psum(right_part, ("dp", "rep"))
    approximation = jnp.concatenate(
        [
            jnp.einsum(
                "kd,kc->dc",
                basis_rows[matrix_id * factor_rank : (matrix_id + 1) * factor_rank],
                new_right[:, bounds[matrix_id][0] : bounds[matrix_id][1]],
                precision=PRECISE,
            )
            for matrix_id in range(4)
        ],
        axis=1,
    )
    new_feedback = (worker_rows - approximation / rep_count)[None]
    new_momentum = MOMENTUM_DECAY * momentum + approximation
    new_weights = text_weights - STEP_RATE * new_momentum
    new_vector_momentum = MOMENTUM_DECAY * vector_momentum + vector_total
    new_vectors = text_vectors - STEP_RATE * new_vector_momentum
    return (
        loss_total,
        text_output,
        grad_inputs,
        new_weights,
        new_momentum,
        new_feedback,
        new_vectors,
        new_vector_momentum,
        left_basis,
        new_right,
    )


def solution(mesh):
    placed = (
        P(("dp", "rep"), None, None),
        P("dp", None),
        P(),
        P(("dp", "rep"), None, None),
        P(("dp", "rep"), None),
        P("dp", None),
        P(),
        P("dp", None),
        P(),
        P("rep", "dp", None),
        P(),
    )
    return jax.shard_map(
        per_device,
        mesh=mesh,
        in_specs=placed,
        out_specs=(
            P(),
            P(("dp", "rep"), None, None),
            P(("dp", "rep"), None, None),
            P("dp", None),
            P("dp", None),
            P("rep", "dp", None),
            P(),
            P(),
            P(),
            P(),
        ),
        check_vma=False,
    )
```

profile of v0, /device:TPU:8, one launch (start us, length us, event | category | flops | bytes accessed | tf_op | source)
XLA Modules:
  0.0 1259.0 jit_solution(4314769996404762950)
XLA Ops:
  8.0 3.5 convert_element_type.126
  14.4 190.8 %all-gather.4.cloned.1.call-done = bf16[768,9216]{1,0:T(8,128)(2,1)} async-done(((bf16[96,9216]{1,0:T(8,128)(2,1)}), bf16[768,9216]{1,0:T(8,128)(2,1)}) %all-gather.4.cloned.1.call-update) | async-done | bytes 14155792 | tf_op jit(solution)/shard_map/all_gather | solution.py:270
  205.2 5.4 fusion.11
  210.5 5.9 reshape.907
  216.4 4.0 fusion.234
  227.4 6.5 fusion.72
  233.9 17.2 %fusion.76 = f32[8,768]{1,0:T(8,128)S(1)} fusion(f32[8,50,768]{2,1,0:T(8,128)S(1)} %get-tuple-element.130, bf16[768,9216]{1,0:T(8,128)(2,1)} %all-gather.4.cloned.1.call-done, f32[8,50,3072]{2,1,0:T(8,128)S(1)} %get-tuple-element.131, f32[3072]{0:T(1024)S(1)} %slice.199, u8[50,3072]{1,0:T(8,128)(4,1)S(1)} %get-tuple-element.11, ...), kind=kOutput, calls=%fused_computation.137 | convolution fusion | flops 1975597056 | bytes 11209728 | tf_op jit(solution)/shard_map/rsf,df->rsd/dot_general | solution.py:107
  251.9 149.9 %all-gather.6.cloned.1.call-done = bf16[768,9216]{1,0:T(8,128)(2,1)} async-done(((bf16[96,9216]{1,0:T(8,128)(2,1)}), bf16[768,9216]{1,0:T(8,128)(2,1)}) %all-gather.6.cloned.1.call-update) | async-done | bytes 14155792 | tf_op jit(solution)/shard_map/all_gather | solution.py:269
  401.8 2.7 fusion.12
  410.8 3.7 fusion.130
  415.8 4.4 multiply_convert_fusion
  420.2 4.3 fusion.84
  425.2 35.1 %all_gather.20 = bf16[256,768]{1,0:T(8,128)(2,1)S(1)} all-gather(bf16[8,768]{1,0:T(8,128)(2,1)S(1)} %multiply_convert_fusion.2), channel_id=1, replica_groups=mesh['dp'=8,'rep'=4] {'dp','rep'}, dimensions={0}, use_global_device_ids=true | all-gather | bytes 405504 | tf_op jit(solution)/shard_map/all_gather | solution.py:292
  460.3 37.8 %all_gather.21 = bf16[256,768]{1,0:T(8,128)(2,1)S(1)} all-gather(bf16[8,768]{1,0:T(8,128)(2,1)S(1)} %copy-done.23), channel_id=1, replica_groups=mesh['dp'=8,'rep'=4] {'dp','rep'}, dimensions={0}, use_global_device_ids=true | all-gather | bytes 405504 | tf_op jit(solution)/shard_map/all_gather | solution.py:291
  500.7 44.9 %all-reduce = f32[256]{0:T(256)S(1)} all-reduce(f32[256]{0:T(256)S(1)} %get-tuple-element.123), channel_id=1, replica_groups=mesh['dp'=8,'rep'=4] {'dp','rep'}, use_global_device_ids=true, to_apply=%add | all-reduce | flops 256 | bytes 2048
  546.5 5.3 convert_reduce_fusion.1
  551.8 5.0 multiply_reduce_fusion.3
  561.8 5.0 convolution_bitcast_fusion
  566.9 5.1 convolution_bitcast_fusion.1
  574.8 2.2 convert_element_type.144
  577.0 4.1 convolution_bitcast_fusion.2
  581.1 19.5 %pad_maximum_fusion = f32[768,9216]{1,0:T(8,128)} fusion(f32[768,3072]{1,0:T(8,128)} %convolution_bitcast_fusion, f32[768,3072]{1,0:T(8,128)} %convolution_bitcast_fusion.1, f32[768,768]{1,0:T(8,128)S(1)} %convolution_bitcast_fusion.3, f32[768,2304]{1,0:T(8,128)} %convolution_bitcast_fusion.2), kind=kLoop, calls=%fused_computation | loop fusion | flops 21233664 | bytes 56623104 | tf_op jit(solution)/shard_map/concatenate | solution.py:334
  602.2 3.4 fusion.230
  607.2 45.5 %all-reduce.1 = (f32[]{:T(128)}, f32[9216]{0:T(1024)}) all-reduce(f32[]{:T(128)S(6)} %div.223, f32[9216]{0:T(1024)S(1)} %constant_dynamic-update-slice_fusion.9), channel_id=1, replica_groups=mesh['dp'=8,'rep'=4] {'dp','rep'}, use_global_device_ids=true, to_apply=%region_24.25 | all-reduce | flops 9217 | bytes 73736 | tf_op jit(solution)/shard_map/psum | solution.py:347
  652.7 395.9 %reduce-scatter.2.cloned.1.call-done = f32[96,9216]{1,0:T(8,128)} async-done(((f32[768,9216]{1,0:T(8,128)}), f32[96,9216]{1,0:T(8,128)}) %reduce-scatter.2.cloned.1.call-update) | async-done | bytes 3538960 | tf_op jit(solution)/shard_map/reduce_scatter | solution.py:333
  1048.6 3.5 bitcast_add_fusion
  1055.3 29.7 %all-gather = bf16[8,96,32]{1,2,0:T(8,128)(2,1)S(1)} all-gather(bf16[1,96,32]{1,2,0:T(8,128)(2,1)S(1)} %maximum_bitcast_fusion), channel_id=1, replica_groups=mesh['dp'=8,'rep'=4] {'dp'}, dimensions={0}, use_global_device_ids=true | all-gather | bytes 55296 | tf_op jit(solution)/shard_map/all_gather | solution.py:345
  1088.7 11.6 psum.29
  1109.8 128.2 %all-reduce.4.cloned.1.call-done = f32[8,9216]{1,0:T(8,128)} async-done(((f32[8,9216]{1,0:T(8,128)}), f32[8,9216]{1,0:T(8,128)}) %all-reduce.4.cloned.1.call-update) | async-done | bytes 294928 | tf_op jit(solution)/shard_map/psum | solution.py:362
  1238.0 2.2 fusion.138
  1240.2 2.1 fusion.140
  1245.5 6.1 multiply_subtract_fusion
  (255 shorter events, 52.1 us)
Async XLA Ops:
  7.2 198.0 %all-gather.4.cloned.1.call-start = ((), (), s32[]{:S(2)}) async-start(), calls=%async_computation.1 | async-start | bytes 15925248 | tf_op jit(solution)/shard_map/all_gather | solution.py:270
  7.9 4.2 copy-start.36
  7.9 4.9 copy-start.18
  7.9 5.5 copy-start.1
  8.0 5.8 copy-start.6
  8.0 393.8 %all-gather.6.cloned.1.call-start = ((), (), s32[]{:S(2)}) async-start(), calls=%async_computation.2 | async-start | bytes 15925248 | tf_op jit(solution)/shard_map/all_gather | solution.py:269
  11.5 1037.0 %reduce-scatter.2.cloned.1.call-start = ((), (), s32[]{:S(2)}) async-start(), calls=%async_computation.3 | async-start | bytes 31850496 | tf_op jit(solution)/shard_map/reduce_scatter | solution.py:333
  13.4 388.4 %copy-start.16 = (f32[768]{0:T(1024)}, f32[768]{0:T(1024)S(1)}, u32[]{:S(2)}) copy-start(f32[768]{0:T(1024)S(1)} %get-tuple-element.112) | copy-start | bytes 9220
  13.4 388.4 %copy-start.24 = (f32[768]{0:T(1024)}, f32[768]{0:T(1024)S(1)}, u32[]{:S(2)}) copy-start(f32[768]{0:T(1024)S(1)} %get-tuple-element.111) | copy-start | bytes 9220
  13.5 388.2 %copy-start.29 = (f32[2,64]{1,0:T(2,128)}, f32[2,64]{1,0:T(2,128)S(1)}, u32[]{:S(2)}) copy-start(f32[2,64]{1,0:T(2,128)S(1)} %broadcast_multiply_fusion.3) | copy-start | bytes 1540
  13.8 196.8 %copy-start.46 = (f32[2,64]{1,0:T(2,128)}, f32[2,64]{1,0:T(2,128)S(1)}, u32[]{:S(2)}) copy-start(f32[2,64]{1,0:T(2,128)S(1)} %fusion.124) | copy-start | bytes 1540
  14.3 387.5 %copy-start.31 = (f32[2,64]{1,0:T(2,128)}, f32[2,64]{1,0:T(2,128)S(1)}, u32[]{:S(2)}) copy-start(f32[2,64]{1,0:T(2,128)S(1)} %fusion.189) | copy-start | bytes 1540
  414.6 5.6 copy-start.50
  420.2 4.4 copy-start.4
  420.2 4.4 copy-start.37
  420.2 4.4 copy-start.43
  420.2 40.1 %copy-start.23 = (bf16[8,768]{1,0:T(8,128)(2,1)S(1)}, bf16[8,768]{1,0:T(8,128)(2,1)}, u32[]{:S(2)}) copy-start(bf16[8,768]{1,0:T(8,128)(2,1)} %multiply_convert_fusion.3) | copy-start | bytes 36868
  420.2 78.6 %copy-start.53 = (s32[8]{0:T(128)S(1)}, s32[8]{0:T(128)}, u32[]{:S(2)}) copy-start(s32[8]{0:T(128)} %iota_add_fusion) | copy-start | bytes 100
  424.6 121.4 %copy-start.14 = (f32[2,64,768]{2,1,0:T(8,128)}, f32[2,64,768]{2,1,0:T(8,128)S(1)}, u32[]{:S(2)}) copy-start(f32[2,64,768]{2,1,0:T(8,128)S(1)} %fusion.84) | copy-start | bytes 1179652
  546.4 5.3 copy-start.21
  546.4 5.3 copy-start.34
  546.5 5.3 copy-start.39
  551.8 5.0 copy-start.12
  551.8 5.0 copy-start.49
  561.8 5.1 copy-start.13
  561.8 5.1 copy-start.22
  561.8 5.1 copy-start.27
  561.8 5.1 copy-start.35
  561.8 5.1 copy-start.40
  600.6 637.4 %all-reduce.4.cloned.1.call-start = ((), (), s32[]{:S(2)}) async-start(), calls=%async_computation.4 | async-start | bytes 589824 | tf_op jit(solution)/shard_map/psum | solution.py:362
  1238.0 7.5 copy-start
  1245.5 6.1 copy-start.11
  (27 other events, 77.6 us)
Sparse Core Ops, SparseCore 0:
  10.2 194.9 all-gather.3
  207.9 193.7 all-gather.5
  600.7 447.8 reduce-scatter.1
  1108.4 129.5 all-reduce.3
where the time goes:
time: 1270 us; the launch traced here: 1260 us
  waiting for transfers between devices  865 us (68%)
  blocking collectives  205 us (16%)
  matrix products  93.6 us (7%)
  other arithmetic  53.1 us (4%)
  local copies, waits for them, and re-layouts  25.4 us (2%)
  between operations  16.5 us (1%)
    reduce_scatter x1, waiting for transfers between devices, per_device(): lax.psum_scatter(jnp.concatenate(blocks, axis=1), 'dp', scatter_dimension...  396 us
    all_gather x1, waiting for transfers between devices, per_device(): lax.all_gather(image_weights, 'dp', axis=0, tiled=True)  191 us
    all_gather x1, waiting for transfers between devices, per_device(): lax.all_gather(text_weights.astype(jnp.bfloat16), 'dp', axis=0, tiled=True)  150 us
    psum x1, waiting for transfers between devices, per_device(): new_right = lax.psum(right_part, ('dp', 'rep'))  128 us
    psum x1, blocking collectives, per_device(): vector_total, loss_total = lax.psum((vector_grad, loss_part), ('dp', 'rep'))  45.5 us
    unnamed x1, blocking collectives  44.9 us
    all_gather x1, blocking collectives, per_device(): lax.all_gather(image_emb, ('dp', 'rep'), axis=0, tiled=True)  37.8 us
    all_gather x1, blocking collectives, per_device(): lax.all_gather(text_emb, ('dp', 'rep'), axis=0, tiled=True)  35.1 us
  transfers between devices with their start and end apart: 4, of which 4 were waited for; matrix products, arithmetic and copies ran while one was open for 5% of the time, Pallas kernels for 0%

commit v1 on v0

--- a/solution.py
+++ b/solution.py
@@ -16,6 +16,22 @@
 STEP_RATE = 0.08
 NORM_FLOOR = 1e-08
 MASKED = -1e30
+
+
+def ring_gather(x, axis, dim):
+    ways, here, step = (lax.axis_size(axis), lax.axis_index(axis), x.shape[dim])
+    shape = [n * ways if d == dim else n for d, n in enumerate(x.shape)]
+    full = lax.dynamic_update_slice_in_dim(jnp.zeros(shape, x.dtype), x, here * step, axis=dim)
+    going_up = going_down = x
+    for far in range(1, ways // 2 + 1):
+        going_up = lax.ppermute(going_up, axis, [(d, (d + 1) % ways) for d in range(ways)])
+        full = lax.dynamic_update_slice_in_dim(full, going_up, (here - far) % ways * step, axis=dim)
+        if 2 * far < ways:
+            going_down = lax.ppermute(going_down, axis, [(d, (d - 1) % ways) for d in range(ways)])
+            full = lax.dynamic_update_slice_in_dim(
+                full, going_down, (here + far) % ways * step, axis=dim
+            )
+    return full
 
 
 def layer_norm(values, layer_gain, layer_shift):
@@ -266,7 +282,7 @@
     factor_rank = start_factors.shape[0]
     bounds = matrix_bounds()
     text_low, frozen = (
-        lax.all_gather(text_weights.astype(jnp.bfloat16), "dp", axis=0, tiled=True),
+        ring_gather(text_weights.astype(jnp.bfloat16), "dp", 0),
         lax.all_gather(image_weights, "dp", axis=0, tiled=True),
     )
     full_mask = jnp.zeros((device_pairs, patches, patches), jnp.int32) == 0

time: 1270 us -> 1330 us (1.047)
  local copies, waits for them, and re-layouts: 25.4 us -> 47.8 us
  waiting for transfers between devices: 865 us -> 885 us
    ppermute x0 -> x7, waiting for transfers between devices: none -> 360 us  [the longest x4 332 us: ring_gather(): lax.ppermute(going_up, axis, [(d, (d + 1) % ways) for d in range(ways)])]
    all_gather x1, waiting for transfers between devices: 191 us -> 0.01 us  [per_device(): lax.all_gather(image_weights, 'dp', axis=0, tiled=True)]
    all_gather x1 -> x0, waiting for transfers between devices: 150 us -> none  [per_device(): lax.all_gather(text_weights.astype(jnp.bfloat16), 'dp', axis=0, tiled=True)]
  transfers between devices with their start and end apart: 4 -> 10, of which waited for: 4 -> 8; matrix products, arithmetic and copies ran while one was open for 5% -> 4% of each run, Pallas kernels for 0% -> 0%
where the time goes in v1:
time: 1330 us; the launch traced here: 1320 us
  waiting for transfers between devices  885 us (67%)
  blocking collectives  206 us (15%)
  matrix products  93.9 us (7%)
  other arithmetic  56.9 us (4%)
  local copies, waits for them, and re-layouts  47.8 us (4%)
  between operations  16.8 us (1%)
    reduce_scatter x1, waiting for transfers between devices, per_device(): lax.psum_scatter(jnp.concatenate(blocks, axis=1), 'dp', scatter_dimension...  395 us
    ppermute x4, waiting for transfers between devices, ring_gather(): lax.ppermute(going_up, axis, [(d, (d + 1) % ways) for d in range(ways)])  332 us
    psum x1, waiting for transfers between devices, per_device(): new_right = lax.psum(right_part, ('dp', 'rep'))  128 us
    psum x1, blocking collectives, per_device(): vector_total, loss_total = lax.psum((vector_grad, loss_part), ('dp', 'rep'))  45.6 us
    unnamed x1, blocking collectives  44.7 us
    all_gather x1, blocking collectives, per_device(): lax.all_gather(image_emb, ('dp', 'rep'), axis=0, tiled=True)  37.7 us
    all_gather x1, blocking collectives, per_device(): lax.all_gather(text_emb, ('dp', 'rep'), axis=0, tiled=True)  36.5 us
    all_gather x1, blocking collectives, per_device(): gathered_rows = lax.all_gather(factor_rows, 'dp', axis=1, tiled=True)  29.7 us
  transfers between devices with their start and end apart: 10, of which 8 were waited for; matrix products, arithmetic and copies ran while one was open for 4% of the time, Pallas kernels for 0%

profile of v1, /device:TPU:8, one launch (start us, length us, event | category | flops | bytes accessed | tf_op | source)
XLA Modules:
  0.0 1317.1 jit_solution(4429269591691125172)
XLA Ops:
  8.0 6.7 broadcast_in_dim.34
  32.0 81.5 %collective-permute-done = bf16[96,9216]{1,0:T(8,128)(2,1)S(1)} collective-permute-done((bf16[96,9216]{1,0:T(8,128)(2,1)}, bf16[96,9216]{1,0:T(8,128)(2,1)S(1)}, u32[]{:S(2)}, u32[]{:S(2)}) %collective-permute-start) | collective-permute-done | bytes 1769504 | tf_op jit(solution)/shard_map/ppermute | solution.py:27
  119.1 105.3 %collective-permute-done.2 = bf16[96,9216]{1,0:T(8,128)(2,1)S(1)} collective-permute-done((bf16[96,9216]{1,0:T(8,128)(2,1)S(1)}, bf16[96,9216]{1,0:T(8,128)(2,1)S(1)}, u32[]{:S(2)}, u32[]{:S(2)}) %collective-permute-start.2) | collective-permute-done | bytes 1769504 | tf_op jit(solution)/shard_map/ppermute | solution.py:27
  226.8 17.9 %collective-permute-done.3 = bf16[96,9216]{1,0:T(8,128)(2,1)S(1)} collective-permute-done((bf16[96,9216]{1,0:T(8,128)(2,1)S(1)}, bf16[96,9216]{1,0:T(8,128)(2,1)S(1)}, u32[]{:S(2)}, u32[]{:S(2)}) %collective-permute-start.3) | collective-permute-done | bytes 1769504 | tf_op jit(solution)/shard_map/ppermute | solution.py:30
  247.5 93.2 %collective-permute-done.4 = bf16[96,9216]{1,0:T(8,128)(2,1)S(1)} collective-permute-done((bf16[96,9216]{1,0:T(8,128)(2,1)S(1)}, bf16[96,9216]{1,0:T(8,128)(2,1)S(1)}, u32[]{:S(2)}, u32[]{:S(2)}) %collective-permute-start.4) | collective-permute-done | bytes 1769504 | tf_op jit(solution)/shard_map/ppermute | solution.py:27
  344.6 10.2 collective-permute-done.5
  356.1 52.3 %collective-permute-done.6 = bf16[96,9216]{1,0:T(8,128)(2,1)S(1)} collective-permute-done((bf16[96,9216]{1,0:T(8,128)(2,1)S(1)}, bf16[96,9216]{1,0:T(8,128)(2,1)S(1)}, u32[]{:S(2)}, u32[]{:S(2)}) %collective-permute-start.6) | collective-permute-done | bytes 1769504 | tf_op jit(solution)/shard_map/ppermute | solution.py:27
  418.9 3.8 fusion.130
  423.8 4.4 multiply_convert_fusion
  428.3 4.3 fusion.84
  433.5 36.5 %all_gather.16 = bf16[256,768]{1,0:T(8,128)(2,1)S(1)} all-gather(bf16[8,768]{1,0:T(8,128)(2,1)S(1)} %multiply_convert_fusion.2), channel_id=1, replica_groups=mesh['dp'=8,'rep'=4] {'dp','rep'}, dimensions={0}, use_global_device_ids=true | all-gather | bytes 405504 | tf_op jit(solution)/shard_map/all_gather | solution.py:308
  470.0 5.5 fusion.11
  475.5 5.9 reshape.907
  481.4 3.4 fusion.234
  495.1 6.4 fusion.72
  501.6 17.2 %fusion.76 = f32[8,768]{1,0:T(8,128)S(1)} fusion(f32[8,50,768]{2,1,0:T(8,128)S(1)} %get-tuple-element.132, bf16[768,9216]{1,0:T(8,128)(2,1)} %all-gather.3.cloned.1.call-done, f32[8,50,3072]{2,1,0:T(8,128)S(1)} %get-tuple-element.133, f32[3072]{0:T(1024)S(1)} %copy-done.44, u8[50,3072]{1,0:T(8,128)(4,1)S(1)} %get-tuple-element.11, ...), kind=kOutput, calls=%fused_computation.137 | convolution fusion | flops 1975597056 | bytes 11209728 | tf_op jit(solution)/shard_map/rsf,df->rsd/dot_general | solution.py:123
  518.9 37.7 %all_gather.17 = bf16[256,768]{1,0:T(8,128)(2,1)S(1)} all-gather(bf16[8,768]{1,0:T(8,128)(2,1)S(1)} %multiply_convert_fusion.3), channel_id=1, replica_groups=mesh['dp'=8,'rep'=4] {'dp','rep'}, dimensions={0}, use_global_device_ids=true | all-gather | bytes 405504 | tf_op jit(solution)/shard_map/all_gather | solution.py:307
  559.2 44.7 %all-reduce = f32[256]{0:T(256)S(1)} all-reduce(f32[256]{0:T(256)S(1)} %get-tuple-element.125), channel_id=1, replica_groups=mesh['dp'=8,'rep'=4] {'dp','rep'}, use_global_device_ids=true, to_apply=%add | all-reduce | flops 256 | bytes 2048
  604.8 5.3 convert_reduce_fusion.1
  610.1 5.0 multiply_reduce_fusion.3
  620.1 5.0 convolution_bitcast_fusion
  625.2 5.1 convolution_bitcast_fusion.1
  635.3 4.1 convolution_bitcast_fusion.2
  639.4 19.5 %pad_maximum_fusion = f32[768,9216]{1,0:T(8,128)} fusion(f32[768,3072]{1,0:T(8,128)} %convolution_bitcast_fusion, f32[768,3072]{1,0:T(8,128)} %convolution_bitcast_fusion.1, f32[768,768]{1,0:T(8,128)S(1)} %convolution_bitcast_fusion.3, f32[768,2304]{1,0:T(8,128)} %convolution_bitcast_fusion.2), kind=kLoop, calls=%fused_computation | loop fusion | flops 21233664 | bytes 56623104 | tf_op jit(solution)/shard_map/concatenate | solution.py:350
  660.5 3.4 fusion.230
  665.5 45.6 %all-reduce.1 = (f32[]{:T(128)}, f32[9216]{0:T(1024)}) all-reduce(f32[]{:T(128)S(6)} %div.223, f32[9216]{0:T(1024)S(1)} %constant_dynamic-update-slice_fusion.9), channel_id=1, replica_groups=mesh['dp'=8,'rep'=4] {'dp','rep'}, use_global_device_ids=true, to_apply=%region_24.25 | all-reduce | flops 9217 | bytes 73736 | tf_op jit(solution)/shard_map/psum | solution.py:363
  711.1 395.3 %reduce-scatter.2.cloned.1.call-done = f32[96,9216]{1,0:T(8,128)} async-done(((f32[768,9216]{1,0:T(8,128)}), f32[96,9216]{1,0:T(8,128)}) %reduce-scatter.2.cloned.1.call-update) | async-done | bytes 3538960 | tf_op jit(solution)/shard_map/reduce_scatter | solution.py:349
  1106.4 3.5 bitcast_add_fusion
  1113.2 29.7 %all-gather = bf16[8,96,32]{1,2,0:T(8,128)(2,1)S(1)} all-gather(bf16[1,96,32]{1,2,0:T(8,128)(2,1)S(1)} %maximum_bitcast_fusion), channel_id=1, replica_groups=mesh['dp'=8,'rep'=4] {'dp'}, dimensions={0}, use_global_device_ids=true | all-gather | bytes 55296 | tf_op jit(solution)/shard_map/all_gather | solution.py:361
  1146.5 11.6 psum.29
  1167.6 128.2 %all-reduce.4.cloned.1.call-done = f32[8,9216]{1,0:T(8,128)} async-done(((f32[8,9216]{1,0:T(8,128)}), f32[8,9216]{1,0:T(8,128)}) %all-reduce.4.cloned.1.call-update) | async-done | bytes 294928 | tf_op jit(solution)/shard_map/psum | solution.py:378
  1303.3 6.1 multiply_subtract_fusion
  (296 shorter events, 96.0 us)
Async XLA Ops:
  7.2 462.8 %all-gather.3.cloned.1.call-start = ((), (), s32[]{:S(2)}) async-start(), calls=%async_computation.1 | async-start | bytes 15925248 | tf_op jit(solution)/shard_map/all_gather | solution.py:286
  7.9 1098.5 %reduce-scatter.2.cloned.1.call-start = ((), (), s32[]{:S(2)}) async-start(), calls=%async_computation.2 | async-start | bytes 31850496 | tf_op jit(solution)/shard_map/reduce_scatter | solution.py:349
  8.0 6.7 copy-start
  14.7 6.5 copy-start.34
  16.9 96.6 %collective-permute-start = (bf16[96,9216]{1,0:T(8,128)(2,1)}, bf16[96,9216]{1,0:T(8,128)(2,1)S(1)}, u32[]{:S(2)}, u32[]{:S(2)}) collective-permute-start(bf16[96,9216]{1,0:T(8,128)(2,1)} %get-tuple-element.97), channel_id=1, source_target_pairs={{0,4},{4,8},{8,12},{12,16},{16,20},{20,24},{24,28},{28,0},{1,5},{5... | collective-permute-start | bytes 5308424 | tf_op jit(solution)/shard_map/ppermute | solution.py:27
  18.4 97.4 %collective-permute-start.1 = (bf16[96,9216]{1,0:T(8,128)(2,1)}, bf16[96,9216]{1,0:T(8,128)(2,1)S(1)}, u32[]{:S(2)}, u32[]{:S(2)}) collective-permute-start(bf16[96,9216]{1,0:T(8,128)(2,1)} %get-tuple-element.97), channel_id=1, source_target_pairs={{0,28},{4,0},{8,4},{12,8},{16,12},{20,16},{24,20},{28,24},{1,29},{... | collective-permute-start | bytes 5308424 | tf_op jit(solution)/shard_map/ppermute | solution.py:30
  24.7 385.1 %copy-start.17 = (f32[768]{0:T(1024)}, f32[768]{0:T(1024)S(1)}, u32[]{:S(2)}) copy-start(f32[768]{0:T(1024)S(1)} %get-tuple-element.114) | copy-start | bytes 9220
  24.7 385.1 %copy-start.23 = (f32[768]{0:T(1024)}, f32[768]{0:T(1024)S(1)}, u32[]{:S(2)}) copy-start(f32[768]{0:T(1024)S(1)} %get-tuple-element.113) | copy-start | bytes 9220
  26.9 382.9 %copy-start.27 = (f32[2,64]{1,0:T(2,128)}, f32[2,64]{1,0:T(2,128)S(1)}, u32[]{:S(2)}) copy-start(f32[2,64]{1,0:T(2,128)S(1)} %broadcast_multiply_fusion.3) | copy-start | bytes 1540
  28.0 88.4 %copy-start.50 = (f32[2,64]{1,0:T(2,128)}, f32[2,64]{1,0:T(2,128)S(1)}, u32[]{:S(2)}) copy-start(f32[2,64]{1,0:T(2,128)S(1)} %fusion.124) | copy-start | bytes 1540
  29.3 86.6 %copy-start.40 = (f32[8,50]{1,0:T(8,128)}, f32[8,50]{1,0:T(8,128)S(1)}, u32[]{:S(2)}) copy-start(f32[8,50]{1,0:T(8,128)S(1)} %broadcast_multiply_fusion.1) | copy-start | bytes 4804
  30.7 379.1 %copy-start.29 = (f32[2,64]{1,0:T(2,128)}, f32[2,64]{1,0:T(2,128)S(1)}, u32[]{:S(2)}) copy-start(f32[2,64]{1,0:T(2,128)S(1)} %fusion.191) | copy-start | bytes 1540
  113.5 110.9 %collective-permute-start.2 = (bf16[96,9216]{1,0:T(8,128)(2,1)S(1)}, bf16[96,9216]{1,0:T(8,128)(2,1)S(1)}, u32[]{:S(2)}, u32[]{:S(2)}) collective-permute-start(bf16[96,9216]{1,0:T(8,128)(2,1)S(1)} %collective-permute-done), channel_id=1, source_target_pairs={{0,4},{4,8},{8,12},{12,16},{16,20},{20,24},{24,28},{28,0},{1,5},{5... | collective-permute-start | bytes 5308424 | tf_op jit(solution)/shard_map/ppermute | solution.py:27
  115.9 128.9 %collective-permute-start.3 = (bf16[96,9216]{1,0:T(8,128)(2,1)S(1)}, bf16[96,9216]{1,0:T(8,128)(2,1)S(1)}, u32[]{:S(2)}, u32[]{:S(2)}) collective-permute-start(bf16[96,9216]{1,0:T(8,128)(2,1)S(1)} %collective-permute-done.1), channel_id=1, source_target_pairs={{0,28},{4,0},{8,4},{12,8},{16,12},{20,16},{24,20},{28,24},{1,29},{... | collective-permute-start | bytes 5308424 | tf_op jit(solution)/shard_map/ppermute | solution.py:30
  224.3 116.3 %collective-permute-start.4 = (bf16[96,9216]{1,0:T(8,128)(2,1)S(1)}, bf16[96,9216]{1,0:T(8,128)(2,1)S(1)}, u32[]{:S(2)}, u32[]{:S(2)}) collective-permute-start(bf16[96,9216]{1,0:T(8,128)(2,1)S(1)} %collective-permute-done.2), channel_id=1, source_target_pairs={{0,4},{4,8},{8,12},{12,16},{16,20},{20,24},{24,28},{28,0},{1,5},{5... | collective-permute-start | bytes 5308424 | tf_op jit(solution)/shard_map/ppermute | solution.py:27
  244.8 110.0 %collective-permute-start.5 = (bf16[96,9216]{1,0:T(8,128)(2,1)S(1)}, bf16[96,9216]{1,0:T(8,128)(2,1)S(1)}, u32[]{:S(2)}, u32[]{:S(2)}) collective-permute-start(bf16[96,9216]{1,0:T(8,128)(2,1)S(1)} %collective-permute-done.3), channel_id=1, source_target_pairs={{0,28},{4,0},{8,4},{12,8},{16,12},{20,16},{24,20},{28,24},{1,29},{... | collective-permute-start | bytes 5308424 | tf_op jit(solution)/shard_map/ppermute | solution.py:30
  340.7 67.7 %collective-permute-start.6 = (bf16[96,9216]{1,0:T(8,128)(2,1)S(1)}, bf16[96,9216]{1,0:T(8,128)(2,1)S(1)}, u32[]{:S(2)}, u32[]{:S(2)}) collective-permute-start(bf16[96,9216]{1,0:T(8,128)(2,1)S(1)} %collective-permute-done.4), channel_id=1, source_target_pairs={{0,4},{4,8},{8,12},{12,16},{16,20},{20,24},{24,28},{28,0},{1,5},{5... | collective-permute-start | bytes 5308424 | tf_op jit(solution)/shard_map/ppermute | solution.py:27
  344.6 65.2 %copy-start.2 = (bf16[2,64,768]{2,1,0:T(8,128)(2,1)S(1)}, bf16[2,64,768]{2,1,0:T(8,128)(2,1)}, u32[]{:S(2)}) copy-start(bf16[2,64,768]{2,1,0:T(8,128)(2,1)} %param.14) | copy-start | bytes 589828
  422.7 5.6 copy-start.60
  428.3 41.7 %copy-start.41 = (f32[8,50]{1,0:T(8,128)S(1)}, f32[8,50]{1,0:T(8,128)}, u32[]{:S(2)}) copy-start(f32[8,50]{1,0:T(8,128)} %copy-done.40) | copy-start | bytes 4804
  428.3 41.7 %copy-start.46 = (f32[2304]{0:T(1024)S(1)}, f32[2304]{0:T(1024)}, u32[]{:S(2)}) copy-start(f32[2304]{0:T(1024)} %get-tuple-element.124) | copy-start | bytes 27652
  428.3 41.7 %copy-start.58 = (f32[768]{0:T(1024)S(1)}, f32[768]{0:T(1024)}, u32[]{:S(2)}) copy-start(f32[768]{0:T(1024)} %get-tuple-element.121) | copy-start | bytes 9220
  428.3 41.7 %copy-start.59 = (f32[768]{0:T(1024)S(1)}, f32[768]{0:T(1024)}, u32[]{:S(2)}) copy-start(f32[768]{0:T(1024)} %get-tuple-element.122) | copy-start | bytes 9220
  428.3 41.7 %copy-start.61 = (f32[8,50]{1,0:T(8,128)S(1)}, f32[8,50]{1,0:T(8,128)}, u32[]{:S(2)}) copy-start(f32[8,50]{1,0:T(8,128)} %add_rsqrt_fusion.1) | copy-start | bytes 4804
  495.1 6.5 copy-start.54
  501.6 55.8 %copy-start.64 = (s32[8]{0:T(128)S(1)}, s32[8]{0:T(128)}, u32[]{:S(2)}) copy-start(s32[8]{0:T(128)} %iota_add_fusion) | copy-start | bytes 100
  604.8 5.3 copy-start.21
  604.8 5.3 copy-start.32
  604.8 5.3 copy-start.37
  658.9 636.9 %all-reduce.4.cloned.1.call-start = ((), (), s32[]{:S(2)}) async-start(), calls=%async_computation.3 | async-start | bytes 589824 | tf_op jit(solution)/shard_map/psum | solution.py:378
  1295.8 7.5 copy-start.1
  1303.3 6.1 copy-start.12
  (44 other events, 145.6 us)
Sparse Core Ops, SparseCore 0:
  10.2 394.8 all-gather.2
  659.0 447.3 reduce-scatter.1
  1166.3 129.4 all-reduce.3
